TPU v7x, 256 devices: a whole 4x4x8 slice. The times are simulated.
256 devices in a mesh: tm: 32 (over z, x), rows: 8 (over y, core).
Axes of the slice: x: 4, y: 4, z: 8, core: 2. Of those that a mesh axis runs over, the one named last changes fastest.
Arguments:
- observations: float32 [32, 2048], P('tm'), may hold values from -48 to 48
- site_ids: int32 [32, 2048], P('tm'), may hold values from 0 to 4095
- counts: int32 [32], P('tm'), may hold values from 1 to 2048, 49152 in all
- frequencies: float32 [128], replicated, may hold values from -3.140625 to 3.140625
- decay: float32 [128], replicated, may hold values from 0.02 to 0.2
- proc_var: float32 [128], replicated, may hold values from 0.05 to 0.2
Outputs:
- smooth_mean: float32 [32, 256], P('tm', 'rows')
- smooth_cov: float32 [32, 256, 256], P('tm', 'rows')
Inputs may be any that keep to these rules, and one draw needn't show every extreme that they name: Step t observes the sites in its first counts[t] slots; the other slots are ignored.
All inputs are finite; a program needn't handle non-finite values. No bound on the sum of `counts` on one device may be relied on, other than what follows from the above.
Results may differ from a plain program's by a relative error of at most 0.0003.
Values sent between devices are 32-bit elements; how exact they have to be, the bound alone decides.
No kernel may reach another device: no remote copies, remote signals or barrier semaphores. Data moves between devices by JAX's collectives and lax.ppermute only.
A program may use at most 128 MiB of HBM per device.

v0:
```python
import math

import jax
import jax.numpy as jnp
import numpy as np
from jax import lax
from jax.experimental import pallas as pl
from jax.experimental.pallas import tpu as pltpu
from jax.sharding import PartitionSpec as P

GRID = 4096
OBS_VAR = 64
MODES = 128
WIDTH = 2 * MODES
LOW = 32
HIGH = GRID // LOW
CHAIN_LIMIT = 1e-4
FINAL_LIMIT = 1e-2
NEWTON_STEPS = 30

NN = (((1,), (0,)), ((), ()))
NT = (((1,), (1,)), ((), ()))


def tables():
    order = np.arange(MODES, dtype=np.int64)
    high = np.arange(HIGH, dtype=np.int64)
    low = np.arange(LOW, dtype=np.int64)
    turn = 2.0 * math.pi * ((high[:, None] * order[None, :]) % HIGH) / HIGH
    transform = np.concatenate([np.cos(turn), np.sin(turn)], axis=1)
    reverse = MODES - order
    reverse[0] = 2 * MODES
    twiddles = []
    for multiples in (order, order + MODES, reverse, order + 1):
        turn = 2.0 * math.pi * ((low[:, None] * multiples[None, :]) % GRID) / GRID
        twiddles += [np.cos(turn), np.sin(turn)]
    return transform.astype(np.float32), np.stack(twiddles).astype(np.float32)


def dot(left, right, dims=NN):
    return lax.dot_general(left, right, dims, preferred_element_type=jnp.float32)


def exact_dot(left, right, dims=None):
    dims = dims or (((1,), (0,)), ((), ()))
    return lax.dot_general(
        left, right, dims, precision=lax.Precision.HIGHEST, preferred_element_type=jnp.float32
    )


def rounded(array):
    return array.astype(jnp.bfloat16)


def split(array):
    upper = rounded(array)
    return upper, rounded(array - upper.astype(jnp.float32))


def dot3(left, right, dims=NN):
    a_hi, a_lo = left
    b_hi, b_lo = right
    return dot(a_hi, b_hi, dims) + (dot(a_hi, b_lo, dims) + dot(a_lo, b_hi, dims))


def iota(shape, dim):
    return lax.broadcasted_iota(jnp.int32, shape, dim)


def statistics_kernel(count_ref, site_ref, obs_ref, transform_ref, twiddle_ref, out_ref):
    sites = site_ref.shape[1]
    site = site_ref[...]
    live = iota((1, sites), 1) < count_ref[0]
    low = jnp.where(live, site & (LOW - 1), LOW)
    high = site >> (LOW.bit_length() - 1)
    obs = obs_ref[...]
    first = rounded(obs).astype(jnp.float32)
    second = rounded(obs - first).astype(jnp.float32)
    third = obs - first - second
    here = iota((LOW, sites), 0) == low
    zero = jnp.zeros((LOW, sites), jnp.float32)
    stack = jnp.concatenate(
        [
            jnp.where(here, 1.0, zero),
            jnp.where(here, first, zero),
            jnp.where(here, second, zero),
            jnp.where(here, third, zero),
        ],
        axis=0,
    )
    columns = jnp.where(iota((HIGH, sites), 0) == high, 1.0, 0.0)
    binned = dot(rounded(stack), rounded(columns), NT)
    observed = binned[LOW : 2 * LOW] + binned[2 * LOW : 3 * LOW] + binned[3 * LOW :]
    waves = exact_dot(jnp.concatenate([binned[:LOW], observed], axis=0), transform_ref[...])
    real, imag = waves[:LOW, :MODES], waves[:LOW, MODES:]
    real_obs = pltpu.roll(waves[LOW:, :MODES], MODES - 1, 1)
    imag_obs = pltpu.roll(waves[LOW:, MODES:], MODES - 1, 1)
    sources = ((real, imag), (real, imag), (real, -imag), (real_obs, imag_obs))
    for kind, (re, im) in enumerate(sources):
        cosine, sine = twiddle_ref[2 * kind], twiddle_ref[2 * kind + 1]
        out_ref[2 * kind : 2 * kind + 1, :] = jnp.sum(re * cosine - im * sine, 0, keepdims=True)
        out_ref[2 * kind + 1 : 2 * kind + 2, :] = jnp.sum(
            re * sine + im * cosine, 0, keepdims=True
        )


def shear(rows, left):
    row = iota((8, MODES), 0)
    value = jnp.broadcast_to(rows, (8, MODES))
    for bit in (1, 2, 4):
        value = jnp.where((row & bit) != 0, pltpu.roll(value, MODES - bit if left else bit, 1), value)
    return value


def turned(value, amount):
    amount = amount % MODES
    return value if amount == 0 else pltpu.roll(value, amount, 1)


def build_block(stats, phase, block_ref):
    lane_row = iota((1, MODES), 1)
    u_re, u_im = phase[0:1], phase[1:2]
    columns = phase.T
    c_re, c_im = columns[:, 0:1], columns[:, 1:2]
    ahead = [pltpu.roll(stats[i : i + 1], MODES - 2, 1) for i in range(6)]
    inside = lane_row < MODES - 2
    t_re = (shear(stats[0:1], False), shear(stats[4:5], False))
    t_im = (shear(-stats[1:2], False), shear(stats[5:6], False))
    h_re = (
        shear(jnp.where(inside, ahead[0], ahead[2]), True),
        shear(jnp.where(inside, ahead[2], ahead[4]), True),
    )
    h_im = (
        shear(jnp.where(inside, ahead[1], ahead[3]), True),
        shear(jnp.where(inside, ahead[3], ahead[5]), True),
    )
    row, lane = iota((8, MODES), 0), iota((8, MODES), 1)
    for group in range(MODES // 8):
        start = 8 * group
        near = (lane >= row) & (lane < MODES - start)
        tr = turned(jnp.where(near, *t_re), start)
        ti = turned(jnp.where(near, *t_im), start)
        near = (lane >= start) & (lane + row < MODES)
        hr = turned(jnp.where(near, *h_re), -start)
        hi = turned(jnp.where(near, *h_im), -start)
        a_re, a_im = tr * u_re + ti * u_im, ti * u_re - tr * u_im
        b_re, b_im = hr * u_re - hi * u_im, hi * u_re + hr * u_im
        p_re, p_im, m_re, m_im = a_re + b_re, a_im + b_im, a_re - b_re, a_im - b_im
        cr, ci = c_re[start : start + 8], c_im[start : start + 8]
        block_ref[start : start + 8, :MODES] = cr * p_re - ci * p_im
        block_ref[start : start + 8, MODES:] = -(cr * m_im + ci * m_re)
        block_ref[MODES + start : MODES + start + 8, :MODES] = cr * p_im + ci * p_re
        block_ref[MODES + start : MODES + start + 8, MODES:] = cr * m_re - ci * m_im
    scale = MODES / (OBS_VAR * math.sqrt(MODES))
    o_re, o_im = stats[6:7] * scale, stats[7:8] * scale
    return jnp.concatenate([o_re * u_re - o_im * u_im, o_re * u_im + o_im * u_re], axis=1)


def diagonal_mask():
    shape = (MODES, MODES)
    return jnp.where(iota(shape, 0) == iota(shape, 1), 1.0, 0.0)


def spread(row, mask):
    zero = jnp.zeros((MODES, MODES), jnp.float32)
    upper = jnp.concatenate([mask * row[:, :MODES], zero], axis=1)
    return jnp.concatenate([upper, jnp.concatenate([zero, mask * row[:, MODES:]], axis=1)], axis=0)


def diagonal_of(matrix, mask, axis):
    upper = jnp.sum(matrix[:MODES, :MODES] * mask, axis=axis, keepdims=True)
    lower = jnp.sum(matrix[MODES:, MODES:] * mask, axis=axis, keepdims=True)
    return jnp.concatenate([upper, lower], axis=1 - axis)


def off_diagonal(matrix, mask):
    other = 1.0 - mask
    upper = jnp.concatenate([matrix[:MODES, :MODES] * other, matrix[:MODES, MODES:]], axis=1)
    lower = jnp.concatenate([matrix[MODES:, :MODES], matrix[MODES:, MODES:] * other], axis=1)
    return jnp.concatenate([upper, lower], axis=0)


def jacobi(excess, base, mask):
    by_row = lax.rsqrt(base[1] + diagonal_of(excess, mask, 1))
    own = diagonal_of(excess, mask, 0)
    by_lane = lax.rsqrt(base[0] + own)
    scale = by_row * by_lane
    return -off_diagonal(excess, mask) * scale, scale, by_lane, own


def squares(array):
    return jnp.sum(array * array, axis=0, keepdims=True)


def chain_inverse(excess, base, damping, mask):
    residue, scale, by_lane, own = jacobi(excess, base, mask)
    parts = split(residue)
    second = dot3(parts, parts)
    first_two = residue + second
    rest = (first_two + dot(rounded(second), rounded(first_two))) * scale
    diagonal = by_lane * by_lane
    lost = spread(damping[0] * own * diagonal, mask) - rest
    return rest, diagonal, lost, squares(second)


def final_inverse(excess, base, damping, mask):
    residue, scale, by_lane, _ = jacobi(excess, base, mask)
    parts = split(residue)
    second = dot3(parts, parts)
    second_hi = rounded(second)
    near = residue + second + dot(parts[0], second_hi)
    fourth = dot(second_hi, second_hi)
    rest = near + fourth + dot(rounded(near), rounded(fourth))
    return rest * scale, by_lane * by_lane, None, squares(second)


def final_rows(excess, base, rows, mask):
    residue, _, by_lane, _ = jacobi(excess, base, mask)
    parts = split(residue)
    second = dot3(parts, parts)
    second_parts = split(second)
    fourth = rounded(dot(second_parts[0], second_parts[0]))
    value = rows * by_lane
    value = value + dot3(split(value), parts)
    value = value + dot3(split(value), second_parts)
    value = value + dot(rounded(value), fourth)
    return value * by_lane, squares(second)


def product3(left, right, dims=NN):
    return dot3(split(left), split(right), dims)


def eliminate(carried, kept, rest, diagonal, mask, product):
    moved = carried * diagonal + product(carried, rest)
    return moved, moved * kept + product(moved, carried[:WIDTH] - spread(kept, mask), NT)


def solve_kernel(
    place_ref,
    stats_ref,
    frequency_ref,
    decay_ref,
    variance_ref,
    mean_ref,
    cov_ref,
    check_ref,
    phase_ref,
    block1_ref,
    block2_ref,
    rest1_ref,
    rest2_ref,
    lost1_ref,
    lost2_ref,
    saved_ref,
    far_ref,
    carried_ref,
    rows_ref,
    columns_ref,
):
    steps = stats_ref.shape[0]
    half = steps // 2
    time, shard = place_ref[0], place_ref[1]
    flip = time < half
    node = jnp.where(flip, steps - 1 - time, time)
    outer = steps - 1 - node

    def time_of(index):
        return jnp.where(flip, steps - 1 - index, index)

    decays = jnp.exp(-decay_ref[...])
    scale = jnp.sqrt(variance_ref[...] / decays)
    positions = iota((steps, MODES), 0)
    angles = time_of(positions).astype(jnp.float32) * frequency_ref[...]
    cosines = jnp.cos(angles) * (scale / MODES)
    sines = jnp.sin(angles) * (-scale / MODES)
    for index in range(steps):
        phase_ref[index, 0:1, :] = cosines[index : index + 1]
        phase_ref[index, 1:2, :] = sines[index : index + 1]
        phase_ref[index, 2:8, :] = jnp.zeros((6, MODES), jnp.float32)
    twice = jnp.concatenate([decays, decays], axis=1)
    own_base = (1.0 - twice * twice) / twice
    values = (twice, 1.0 / twice, own_base)
    table = jnp.concatenate(values + (jnp.zeros((5, WIDTH), jnp.float32),), axis=0)
    columns_ref[:MODES] = table[:, :MODES].T
    columns_ref[MODES:] = table[:, MODES:].T
    damping, base, own_base = (
        (value, columns_ref[:, i : i + 1]) for i, value in enumerate(values)
    )

    def build(index, block_ref):
        return build_block(stats_ref[time_of(index)], phase_ref[index], block_ref)

    def second_node(index):
        late = jnp.where(index >= half - 1, node, half + index - outer)
        return jnp.where(index < outer, steps - 1 - index, late)

    def run(invert_chain, invert_middle, finish, product):
        mask = diagonal_mask()
        for ref in (rest1_ref, rest2_ref, lost1_ref, lost2_ref, saved_ref, far_ref, carried_ref):
            ref[...] = jnp.zeros(ref.shape, jnp.float32)
        rows_ref[...] = jnp.zeros(rows_ref.shape, jnp.float32)
        check_ref[...] = jnp.zeros(check_ref.shape, jnp.float32)
        rows_ref[8:9, :] = build(0, block1_ref)
        rows_ref[16:17, :] = build(second_node(0), block2_ref)

        def advance(index):
            fresh = index == outer
            excess1 = block1_ref[...] + lost1_ref[...]
            lost2 = lost2_ref[...]
            saved_ref[...] = jnp.where(fresh, lost2, saved_ref[...])
            excess2 = block2_ref[...] + jnp.where(fresh, spread(damping[0], mask), lost2)
            diagonal1, diagonal2 = rows_ref[32:33, :], rows_ref[33:34, :]
            before = rows_ref[0:8, :]
            info1 = rows_ref[8:16, :] + before * diagonal1 + product(before, rest1_ref[...])
            kept = rows_ref[34:35, :]
            moved, left = eliminate(
                carried_ref[...], kept, rest2_ref[...], diagonal2, mask, product
            )
            info2 = moved[WIDTH:]
            rows_ref[34:35, :] = jnp.where(fresh, 1.0, kept * diagonal2)
            rows_ref[24:32, :] = jnp.where(fresh, info2, rows_ref[24:32, :])
            far_ref[...] = jnp.where(fresh, 0.0, far_ref[...] + left)
            ones = jnp.ones((1, WIDTH), jnp.float32)
            carried_ref[:WIDTH] = jnp.where(fresh, spread(ones, mask), moved[:WIDTH])
            info2 = jnp.where(fresh, 0.0, info2) + rows_ref[16:24, :]
            carried_ref[WIDTH:] = info2
            rows_ref[0:8, :] = info1
            return excess1, excess2, info1, info2

        def body(index, _):
            excess1, excess2, _, _ = advance(index)
            next1 = invert_chain(excess1, base, damping, mask)
            next2 = invert_chain(excess2, base, damping, mask)
            rest1_ref[...], rows_ref[32:33, :], lost1_ref[...] = next1
            rest2_ref[...], rows_ref[33:34, :], lost2_ref[...] = next2
            rows_ref[8:9, :] = build(index + 1, block1_ref)
            rows_ref[16:17, :] = build(second_node(index + 1), block2_ref)
            return 0

        lax.fori_loop(0, half - 1, body, 0)
        excess1, excess2, info1, info2 = advance(half - 1)
        rest, diagonal, _ = invert_middle(excess1 - far_ref[:WIDTH], base, damping, mask)
        carried_ref[:WIDTH] = carried_ref[:WIDTH].T
        carried_ref[WIDTH:] = info1 + far_ref[WIDTH:]
        _, left = eliminate(carried_ref[...], rows_ref[34:35, :], rest, diagonal, mask, product)
        excess = excess2 + saved_ref[...] - left[:WIDTH]
        info = info2 + rows_ref[24:32, :] + left[WIDTH:]

        block = cov_ref.shape[0]
        cosine = phase_ref[node, 0:1, :] * MODES
        sine = phase_ref[node, 1:2, :] * (-MODES)
        even = jnp.concatenate([cosine, -sine], axis=1)
        odd = jnp.concatenate([sine, cosine], axis=1)

        def turn_back(rows, start):
            row = iota((rows, WIDTH), 0) + start
            lane = iota((rows, WIDTH), 1) & (MODES - 1)
            value = jnp.where((row & 1) == 0, even, odd)
            return jnp.where(lane == (row >> 1), value, 0.0)

        mine = turn_back(block, shard * block)
        whole = split(turn_back(WIDTH, 0))
        (result,) = finish(excess, own_base, jnp.concatenate([mine, info], axis=0), mask)
        mean_ref[...] = dot3(split(result[block:]), split(mine), NT)[0:1]
        cov_ref[...] = dot3(split(result[:block]), whole, NT)

    def noted(inverse, row):
        def call(*args):
            *value, measure = inverse(*args)
            check_ref[row : row + 1, :] = jnp.maximum(check_ref[row : row + 1, :], measure)
            return value

        return call

    run(noted(chain_inverse, 0), noted(final_inverse, 1), noted(final_rows, 1), product3)


def solve(place, stats, frequencies, decay, proc_var, block):
    square = pltpu.VMEM((WIDTH, WIDTH), jnp.float32)
    tall = pltpu.VMEM((WIDTH + 8, WIDTH), jnp.float32)
    vmem = pl.BlockSpec(memory_space=pltpu.VMEM)
    return pl.pallas_call(
        solve_kernel,
        out_shape=(
            jax.ShapeDtypeStruct((1, block), jnp.float32),
            jax.ShapeDtypeStruct((block, WIDTH), jnp.float32),
            jax.ShapeDtypeStruct((2, WIDTH), jnp.float32),
        ),
        in_specs=[pl.BlockSpec(memory_space=pltpu.SMEM)] + [vmem] * 4,
        out_specs=(vmem, vmem, vmem),
        scratch_shapes=[
            pltpu.VMEM((stats.shape[0], 8, MODES), jnp.float32),
            *[square] * 7,
            tall,
            tall,
            pltpu.VMEM((40, WIDTH), jnp.float32),
            pltpu.VMEM((WIDTH, 8), jnp.float32),
        ],
        compiler_params=pltpu.CompilerParams(vmem_limit_bytes=48 << 20),
        name="solve",
    )(place, stats, frequencies[None], decay[None], proc_var[None])


def newton_inverse(matrix):
    eye = jnp.eye(WIDTH, dtype=jnp.float32)
    start = eye / jnp.sum(jnp.abs(matrix), axis=1, keepdims=True)

    def step(_, approx):
        return approx + exact_dot(approx, eye - exact_dot(matrix, approx))

    return lax.fori_loop(0, NEWTON_STEPS, step, start)


def general(place, stats, frequencies, decay, proc_var, block):
    steps = stats.shape[0]
    time, shard = place[0], place[1]
    damping = jnp.exp(-decay)
    scale = jnp.sqrt(proc_var / damping)
    twice = jnp.concatenate([damping, damping])
    order = jnp.arange(1, MODES + 1)
    apart, together = order[:, None] - order[None, :], order[:, None] + order[None, :]
    direction = jnp.sign(apart).astype(jnp.float32)

    def node(index):
        rows = stats[index]
        even = jnp.concatenate([rows[0], rows[2], rows[4, :1]])
        odd = jnp.concatenate([rows[1], rows[3], rows[5, :1]])
        angle = index.astype(jnp.float32) * frequencies
        u_re, u_im = scale / MODES * jnp.cos(angle), -scale / MODES * jnp.sin(angle)
        t_re, t_im = even[jnp.abs(apart)], direction * odd[jnp.abs(apart)]
        h_re, h_im = even[together], odd[together]
        a_re, a_im = t_re * u_re + t_im * u_im, t_im * u_re - t_re * u_im
        b_re, b_im = h_re * u_re - h_im * u_im, h_im * u_re + h_re * u_im
        c_re, c_im = u_re[:, None], u_im[:, None]
        p_re, p_im, m_re, m_im = a_re + b_re, a_im + b_im, a_re - b_re, a_im - b_im
        upper = jnp.concatenate([c_re * p_re - c_im * p_im, -(c_re * m_im + c_im * m_re)], axis=1)
        lower = jnp.concatenate([c_re * p_im + c_im * p_re, c_re * m_re - c_im * m_im], axis=1)
        factor = MODES / (OBS_VAR * math.sqrt(MODES))
        o_re, o_im = rows[6] * factor, rows[7] * factor
        info = jnp.concatenate([o_re * u_re - o_im * u_im, o_re * u_im + o_im * u_re])
        return jnp.concatenate([upper, lower], axis=0), info

    def passed(index, state):
        lost, message = state
        precision, info = node(index)
        excess = precision + lost
        inverse = newton_inverse(jnp.diag(1.0 / twice) + excess)
        lost = twice[:, None] * exact_dot(excess, inverse)
        return 0.5 * (lost + lost.T), exact_dot(inverse, info + message)

    start = (jnp.zeros((WIDTH, WIDTH), jnp.float32), jnp.zeros((WIDTH,), jnp.float32))
    before = lax.fori_loop(0, time, passed, start)
    after = lax.fori_loop(
        0, steps - 1 - time, lambda index, state: passed(steps - 1 - index, state), start
    )
    precision, info = node(time)
    base = jnp.diag((1.0 - twice * twice) / twice)
    inverse = newton_inverse(base + precision + before[0] + after[0])
    angle = time.astype(jnp.float32) * frequencies
    cosine, sine = jnp.diag(scale * jnp.cos(angle)), jnp.diag(scale * jnp.sin(angle))
    back = jnp.stack(
        [jnp.concatenate([cosine, -sine], axis=1), jnp.concatenate([sine, cosine], axis=1)], axis=1
    ).reshape(WIDTH, WIDTH)
    mine = exact_dot(lax.dynamic_slice_in_dim(back, shard * block, block, 0), inverse)
    mean = exact_dot(mine, info + before[1] + after[1])
    return mean[None], exact_dot(mine, back, NT)


def statistics(site_row, obs_row, count):
    transform, twiddles = tables()
    vmem = pl.BlockSpec(memory_space=pltpu.VMEM)
    return pl.pallas_call(
        statistics_kernel,
        out_shape=jax.ShapeDtypeStruct((8, MODES), jnp.float32),
        in_specs=[pl.BlockSpec(memory_space=pltpu.SMEM)] + [vmem] * 4,
        out_specs=vmem,
        name="statistics",
    )(count, site_row, obs_row, jnp.asarray(transform), jnp.asarray(twiddles))


def local(observations, site_ids, counts, frequencies, decay, proc_var):
    steps = lax.axis_size("tm")
    block = WIDTH // lax.axis_size("rows")
    stats = statistics(site_ids, observations, counts)
    copies = jnp.broadcast_to(stats, (steps, *stats.shape))
    everyone = lax.all_to_all(copies, "tm", split_axis=0, concat_axis=0, tiled=True)
    place = jnp.stack([lax.axis_index("tm"), lax.axis_index("rows")]).astype(jnp.int32)
    mean, cov, check = solve(place, everyone, frequencies, decay, proc_var, block)
    measure = jnp.sum(check, axis=1)
    mean, cov = lax.cond(
        (measure[0] <= CHAIN_LIMIT) & (measure[1] <= FINAL_LIMIT),
        lambda place, everyone, mean, cov: (mean, cov),
        lambda place, everyone, mean, cov: general(
            place, everyone, frequencies, decay, proc_var, block
        ),
        place,
        everyone,
        mean,
        cov,
    )
    return mean, cov[None]


def solution(mesh):
    return jax.shard_map(
        local,
        mesh=mesh,
        in_specs=(P("tm", None), P("tm", None), P("tm"), P(), P(), P()),
        out_specs=(P("tm", "rows"), P("tm", "rows", None)),
        check_vma=False,
    )
```

profile of v0, /device:TPU:16, one launch (start us, length us, event | category | flops | bytes accessed | tf_op | source)
XLA Modules:
  0.0 76.1 jit_solution(12019048219920276146)
XLA Ops:
  1.3 2.2 %statistics.1 = f32[8,128]{1,0:T(8,128)} custom-call(s32[1]{0:T(128)S(6)} %copy.79.count_ref, s32[1,2048]{1,0:T(1,128)} %site_ref.1, f32[1,2048]{1,0:T(1,128)} %obs_ref.1, f32[128,256]{1,0:T(8,128)} %constant.167.clone.transform_ref, f32[8,32,128]{2,1,0:T(8,128)} %constant.168.clone.twiddle_ref), custom_call_target="tpu_custom_call" | custom-call | tf_op jit(solution)/shard_map/statistics/pallas_call | solution.py:473
  3.5 1.3 %broadcast_in_dim.155 = f32[32,8,128]{2,1,0:T(8,128)} broadcast(f32[8,128]{1,0:T(8,128)} %statistics.1), dimensions={1,2} | broadcast | bytes 135168 | tf_op jit(solution)/shard_map/broadcast_in_dim | solution.py:486
  4.9 11.3 %all-to-all-start = ((f32[32,8,128]{2,1,0:T(8,128)}), f32[32,8,128]{2,1,0:T(8,128)S(1)}, u32[]{:S(2)}, u32[]{:S(2)}) async-start(f32[32,8,128]{2,1,0:T(8,128)} %broadcast_in_dim.155), calls=%async_computation | async-start | bytes 262144 | tf_op jit(solution)/shard_map/all_to_all | solution.py:487
  16.2 0.1 pad_add_fusion.place_ref
  16.3 10.4 %all-to-all-done.stats_ref = f32[32,8,128]{2,1,0:T(8,128)S(1)} async-done(((f32[32,8,128]{2,1,0:T(8,128)}), f32[32,8,128]{2,1,0:T(8,128)S(1)}, u32[]{:S(2)}, u32[]{:S(2)}) %all-to-all-start) | async-done | bytes 131104 | tf_op jit(solution)/shard_map/all_to_all | solution.py:487
  26.6 0.0 copy-start.2
  26.6 0.0 copy-start.12
  26.6 0.0 copy-start.13
  26.6 0.6 copy-done.2
  27.3 0.0 copy-done.12
  27.3 0.0 copy-done.13
  27.3 46.3 %solve.1 = (f32[1,32]{1,0:T(1,128)}, f32[32,256]{1,0:T(8,128)}, f32[2,256]{1,0:T(2,128)S(1)}) custom-call(s32[2]{0:T(128)S(1)} %pad_add_fusion.place_ref, f32[32,8,128]{2,1,0:T(8,128)S(1)} %all-to-all-done.stats_ref, f32[1,128]{1,0:T(1,128)S(1)} %bitcast.375, f32[1,128]{1,0:T(1,128)S(1)} %bitcast.379, f32[1,128]{1,0:T(1,128)S(1)} %bitcast.380), custom_call_target="tpu_custom_call" | custom-call | tf_op jit(solution)/shard_map/solve/pallas_call | solution.py:383
  73.6 0.1 reduce_sum.41
  73.8 0.6 fusion.82
  75.6 0.2 conditional.1
Async XLA Ops:
  4.9 21.8 %all-to-all-start = ((f32[32,8,128]{2,1,0:T(8,128)}), f32[32,8,128]{2,1,0:T(8,128)S(1)}, u32[]{:S(2)}, u32[]{:S(2)}) async-start(f32[32,8,128]{2,1,0:T(8,128)} %broadcast_in_dim.155), calls=%async_computation | async-start | bytes 262144 | tf_op jit(solution)/shard_map/all_to_all | solution.py:487
  26.6 0.7 copy-start.2
  26.6 0.7 copy-start.12
  26.6 0.7 copy-start.13
where the time goes:
time: 76.3 us; the launch traced here: 76.1 us
  Pallas kernels  48.6 us (64%)
  starting transfers between devices  11.3 us (15%)
  waiting for transfers between devices  10.4 us (14%)
  between operations  2.75 us (4%)
  local copies, waits for them, and re-layouts  2.64 us (3%)
    pallas_call x1, Pallas kernels, solve(): pl.pallas_call(solve_kernel, out_shape=(jax.ShapeDtypeStruct((1, block),...  46.3 us
    all_to_all x1, starting transfers between devices, local(): lax.all_to_all(copies, 'tm', split_axis=0, concat_axis=0, tiled=True)  11.3 us
    all_to_all x1, waiting for transfers between devices, local(): lax.all_to_all(copies, 'tm', split_axis=0, concat_axis=0, tiled=True)  10.4 us
    pallas_call x1, Pallas kernels, statistics(): pl.pallas_call(statistics_kernel, out_shape=jax.ShapeDtypeStruct((8, MODE...  2.23 us
  transfers between devices with their start and end apart: 1, of which 1 were waited for; matrix products, arithmetic and copies ran while one was open for 0% of the time, Pallas kernels for 0%

commit v1 on v0

--- a/solution.py
+++ b/solution.py
@@ -28,10 +28,10 @@
     low = np.arange(LOW, dtype=np.int64)
     turn = 2.0 * math.pi * ((high[:, None] * order[None, :]) % HIGH) / HIGH
     transform = np.concatenate([np.cos(turn), np.sin(turn)], axis=1)
-    reverse = MODES - order
-    reverse[0] = 2 * MODES
+    far_back = 2 * MODES + 1 - order
+    far_back[0] = MODES + 1
     twiddles = []
-    for multiples in (order, order + MODES, reverse, order + 1):
+    for multiples in (order, far_back, MODES - order, order + 1):
         turn = 2.0 * math.pi * ((low[:, None] * multiples[None, :]) % GRID) / GRID
         twiddles += [np.cos(turn), np.sin(turn)]
     return transform.astype(np.float32), np.stack(twiddles).astype(np.float32)
@@ -60,7 +60,12 @@
 def dot3(left, right, dims=NN):
     a_hi, a_lo = left
     b_hi, b_lo = right
-    return dot(a_hi, b_hi, dims) + (dot(a_hi, b_lo, dims) + dot(a_lo, b_hi, dims))
+    (left_dim,), (right_dim,) = dims[0]
+    return dot(
+        jnp.concatenate([a_hi, a_hi, a_lo], axis=left_dim),
+        jnp.concatenate([b_hi, b_lo, b_hi], axis=right_dim),
+        dims,
+    )
 
 
 def iota(shape, dim):
@@ -95,7 +100,8 @@
     real, imag = waves[:LOW, :MODES], waves[:LOW, MODES:]
     real_obs = pltpu.roll(waves[LOW:, :MODES], MODES - 1, 1)
     imag_obs = pltpu.roll(waves[LOW:, MODES:], MODES - 1, 1)
-    sources = ((real, imag), (real, imag), (real, -imag), (real_obs, imag_obs))
+    turned = (pltpu.roll(real, 1, 1), pltpu.roll(-imag, 1, 1))
+    sources = ((real, imag), turned, (real, -imag), (real_obs, imag_obs))
     for kind, (re, im) in enumerate(sources):
         cosine, sine = twiddle_ref[2 * kind], twiddle_ref[2 * kind + 1]
         out_ref[2 * kind : 2 * kind + 1, :] = jnp.sum(re * cosine - im * sine, 0, keepdims=True)
@@ -104,53 +110,39 @@
         )
 
 
-def shear(rows, left):
-    row = iota((8, MODES), 0)
-    value = jnp.broadcast_to(rows, (8, MODES))
-    for bit in (1, 2, 4):
-        value = jnp.where((row & bit) != 0, pltpu.roll(value, MODES - bit if left else bit, 1), value)
-    return value
-
-
-def turned(value, amount):
-    amount = amount % MODES
-    return value if amount == 0 else pltpu.roll(value, amount, 1)
+def toeplitz(ahead, behind):
+    shape = (MODES, MODES)
+    upper = pltpu.roll(jnp.broadcast_to(ahead, shape), 0, 1, stride=1, stride_axis=0)
+    lower = pltpu.roll(jnp.broadcast_to(behind, shape), 0, 1, stride=1, stride_axis=0)
+    return jnp.where(iota(shape, 1) >= iota(shape, 0), upper, lower)
 
 
 def build_block(stats, phase, block_ref):
-    lane_row = iota((1, MODES), 1)
     u_re, u_im = phase[0:1], phase[1:2]
     columns = phase.T
-    c_re, c_im = columns[:, 0:1], columns[:, 1:2]
-    ahead = [pltpu.roll(stats[i : i + 1], MODES - 2, 1) for i in range(6)]
-    inside = lane_row < MODES - 2
-    t_re = (shear(stats[0:1], False), shear(stats[4:5], False))
-    t_im = (shear(-stats[1:2], False), shear(stats[5:6], False))
-    h_re = (
-        shear(jnp.where(inside, ahead[0], ahead[2]), True),
-        shear(jnp.where(inside, ahead[2], ahead[4]), True),
-    )
-    h_im = (
-        shear(jnp.where(inside, ahead[1], ahead[3]), True),
-        shear(jnp.where(inside, ahead[3], ahead[5]), True),
-    )
-    row, lane = iota((8, MODES), 0), iota((8, MODES), 1)
-    for group in range(MODES // 8):
-        start = 8 * group
-        near = (lane >= row) & (lane < MODES - start)
-        tr = turned(jnp.where(near, *t_re), start)
-        ti = turned(jnp.where(near, *t_im), start)
-        near = (lane >= start) & (lane + row < MODES)
-        hr = turned(jnp.where(near, *h_re), -start)
-        hi = turned(jnp.where(near, *h_im), -start)
-        a_re, a_im = tr * u_re + ti * u_im, ti * u_re - tr * u_im
-        b_re, b_im = hr * u_re - hi * u_im, hi * u_re + hr * u_im
-        p_re, p_im, m_re, m_im = a_re + b_re, a_im + b_im, a_re - b_re, a_im - b_im
-        cr, ci = c_re[start : start + 8], c_im[start : start + 8]
-        block_ref[start : start + 8, :MODES] = cr * p_re - ci * p_im
-        block_ref[start : start + 8, MODES:] = -(cr * m_im + ci * m_re)
-        block_ref[MODES + start : MODES + start + 8, :MODES] = cr * p_im + ci * p_re
-        block_ref[MODES + start : MODES + start + 8, MODES:] = cr * m_re - ci * m_im
+    cr, ci = columns[:, 0:1], columns[:, 1:2]
+    tr = toeplitz(stats[0:1], stats[4:5])
+    ti = toeplitz(-stats[1:2], stats[5:6])
+    start = iota((1, MODES), 1) == 0
+    near = [
+        jnp.where(start, stats[2 + i : 3 + i], pltpu.roll(stats[4 + i : 5 + i], 1, 1))
+        for i in range(2)
+    ]
+    mirrored = jnp.concatenate(
+        [toeplitz(near[0], stats[2:3]), toeplitz(near[1], stats[3:4])], axis=0
+    )
+    shape = (2 * MODES, MODES)
+    row = iota(shape, 0) & (MODES - 1)
+    mirror = rounded(jnp.where(row + iota(shape, 1) == MODES - 1, 1.0, 0.0))
+    sums = dot(jnp.concatenate(split(mirrored), axis=1), mirror)
+    hr, hi = sums[:MODES], sums[MODES:]
+    a_re, a_im = tr * u_re + ti * u_im, ti * u_re - tr * u_im
+    b_re, b_im = hr * u_re - hi * u_im, hi * u_re + hr * u_im
+    p_re, p_im, m_re, m_im = a_re + b_re, a_im + b_im, a_re - b_re, a_im - b_im
+    block_ref[:MODES, :MODES] = cr * p_re - ci * p_im
+    block_ref[:MODES, MODES:] = -(cr * m_im + ci * m_re)
+    block_ref[MODES:, :MODES] = cr * p_im + ci * p_re
+    block_ref[MODES:, MODES:] = cr * m_re - ci * m_im
     scale = MODES / (OBS_VAR * math.sqrt(MODES))
     o_re, o_im = stats[6:7] * scale, stats[7:8] * scale
     return jnp.concatenate([o_re * u_re - o_im * u_im, o_re * u_im + o_im * u_re], axis=1)
@@ -297,6 +289,7 @@
 
     def run(invert_chain, invert_middle, finish, product):
         mask = diagonal_mask()
+        ones = jnp.ones((1, WIDTH), jnp.float32)
         for ref in (rest1_ref, rest2_ref, lost1_ref, lost2_ref, saved_ref, far_ref, carried_ref):
             ref[...] = jnp.zeros(ref.shape, jnp.float32)
         rows_ref[...] = jnp.zeros(rows_ref.shape, jnp.float32)
@@ -305,11 +298,22 @@
         rows_ref[16:17, :] = build(second_node(0), block2_ref)
 
         def advance(index):
-            fresh = index == outer
+            @pl.when(index == outer)
+            def _():
+                message = carried_ref[WIDTH:]
+                saved_ref[...] = lost2_ref[...]
+                rows_ref[24:32, :] = message * rows_ref[33:34, :] + product(message, rest2_ref[...])
+                eye = spread(ones, mask)
+                lost2_ref[...] = spread(damping[0], mask)
+                rest2_ref[...] = jnp.zeros((WIDTH, WIDTH), jnp.float32)
+                rows_ref[33:35, :] = jnp.ones((2, WIDTH), jnp.float32)
+                carried_ref[:WIDTH] = eye
+                carried_ref[WIDTH:] = jnp.zeros((8, WIDTH), jnp.float32)
+                far_ref[:WIDTH] = -eye
+                far_ref[WIDTH:] = jnp.zeros((8, WIDTH), jnp.float32)
+
             excess1 = block1_ref[...] + lost1_ref[...]
-            lost2 = lost2_ref[...]
-            saved_ref[...] = jnp.where(fresh, lost2, saved_ref[...])
-            excess2 = block2_ref[...] + jnp.where(fresh, spread(damping[0], mask), lost2)
+            excess2 = block2_ref[...] + lost2_ref[...]
             diagonal1, diagonal2 = rows_ref[32:33, :], rows_ref[33:34, :]
             before = rows_ref[0:8, :]
             info1 = rows_ref[8:16, :] + before * diagonal1 + product(before, rest1_ref[...])
@@ -317,13 +321,10 @@
             moved, left = eliminate(
                 carried_ref[...], kept, rest2_ref[...], diagonal2, mask, product
             )
-            info2 = moved[WIDTH:]
-            rows_ref[34:35, :] = jnp.where(fresh, 1.0, kept * diagonal2)
-            rows_ref[24:32, :] = jnp.where(fresh, info2, rows_ref[24:32, :])
-            far_ref[...] = jnp.where(fresh, 0.0, far_ref[...] + left)
-            ones = jnp.ones((1, WIDTH), jnp.float32)
-            carried_ref[:WIDTH] = jnp.where(fresh, spread(ones, mask), moved[:WIDTH])
-            info2 = jnp.where(fresh, 0.0, info2) + rows_ref[16:24, :]
+            rows_ref[34:35, :] = kept * diagonal2
+            far_ref[...] += left
+            carried_ref[:WIDTH] = moved[:WIDTH]
+            info2 = moved[WIDTH:] + rows_ref[16:24, :]
             carried_ref[WIDTH:] = info2
             rows_ref[0:8, :] = info1
             return excess1, excess2, info1, info2
@@ -424,8 +425,8 @@
 
     def node(index):
         rows = stats[index]
-        even = jnp.concatenate([rows[0], rows[2], rows[4, :1]])
-        odd = jnp.concatenate([rows[1], rows[3], rows[5, :1]])
+        even = jnp.concatenate([rows[0], rows[4, :1], rows[2, :1], rows[2, :0:-1]])
+        odd = jnp.concatenate([rows[1], rows[5, :1], rows[3, :1], rows[3, :0:-1]])
         angle = index.astype(jnp.float32) * frequencies
         u_re, u_im = scale / MODES * jnp.cos(angle), -scale / MODES * jnp.sin(angle)
         t_re, t_im = even[jnp.abs(apart)], direction * odd[jnp.abs(apart)]

time: 76.3 us -> 56.6 us (0.74)
  Pallas kernels: 48.6 us -> 28.9 us
    pallas_call x1, Pallas kernels: 46.3 us -> 26.6 us  [solve(): pl.pallas_call(solve_kernel, out_shape=(jax.ShapeDtypeStruct((1, block),...]
where the time goes in v1:
time: 56.6 us; the launch traced here: 56.3 us
  Pallas kernels  28.9 us (51%)
  starting transfers between devices  11.3 us (20%)
  waiting for transfers between devices  10.4 us (18%)
  between operations  2.74 us (5%)
  local copies, waits for them, and re-layouts  2.63 us (5%)
    pallas_call x1, Pallas kernels, solve(): pl.pallas_call(solve_kernel, out_shape=(jax.ShapeDtypeStruct((1, block),...  26.6 us
    all_to_all x1, starting transfers between devices, local(): lax.all_to_all(copies, 'tm', split_axis=0, concat_axis=0, tiled=True)  11.3 us
    all_to_all x1, waiting for transfers between devices, local(): lax.all_to_all(copies, 'tm', split_axis=0, concat_axis=0, tiled=True)  10.4 us
    pallas_call x1, Pallas kernels, statistics(): pl.pallas_call(statistics_kernel, out_shape=jax.ShapeDtypeStruct((8, MODE...  2.24 us
    broadcast_in_dim x1, local copies, waits for them, and re-layouts, local(): copies = jnp.broadcast_to(stats, (steps, *stats.shape))  1.34 us
  transfers between devices with their start and end apart: 1, of which 1 were waited for; matrix products, arithmetic and copies ran while one was open for 0% of the time, Pallas kernels for 0%

profile of v1, /device:TPU:16, one launch (start us, length us, event | category | flops | bytes accessed | tf_op | source)
XLA Modules:
  0.0 56.3 jit_solution(9475233084245932612)
XLA Ops:
  1.3 2.2 %statistics.1 = f32[8,128]{1,0:T(8,128)} custom-call(s32[1]{0:T(128)S(6)} %copy.79.count_ref, s32[1,2048]{1,0:T(1,128)} %site_ref.1, f32[1,2048]{1,0:T(1,128)} %obs_ref.1, f32[128,256]{1,0:T(8,128)} %constant.167.clone.transform_ref, f32[8,32,128]{2,1,0:T(8,128)} %constant.168.clone.twiddle_ref), custom_call_target="tpu_custom_call" | custom-call | tf_op jit(solution)/shard_map/statistics/pallas_call | solution.py:474
  3.5 1.3 %broadcast_in_dim.155 = f32[32,8,128]{2,1,0:T(8,128)} broadcast(f32[8,128]{1,0:T(8,128)} %statistics.1), dimensions={1,2} | broadcast | bytes 135168 | tf_op jit(solution)/shard_map/broadcast_in_dim | solution.py:487
  4.9 11.3 %all-to-all-start = ((f32[32,8,128]{2,1,0:T(8,128)}), f32[32,8,128]{2,1,0:T(8,128)S(1)}, u32[]{:S(2)}, u32[]{:S(2)}) async-start(f32[32,8,128]{2,1,0:T(8,128)} %broadcast_in_dim.155), calls=%async_computation | async-start | bytes 262144 | tf_op jit(solution)/shard_map/all_to_all | solution.py:488
  16.2 0.1 pad_add_fusion.place_ref
  16.3 10.4 %all-to-all-done.stats_ref = f32[32,8,128]{2,1,0:T(8,128)S(1)} async-done(((f32[32,8,128]{2,1,0:T(8,128)}), f32[32,8,128]{2,1,0:T(8,128)S(1)}, u32[]{:S(2)}, u32[]{:S(2)}) %all-to-all-start) | async-done | bytes 131104 | tf_op jit(solution)/shard_map/all_to_all | solution.py:488
  26.6 0.0 copy-start.2
  26.6 0.0 copy-start.11
  26.6 0.0 copy-start.12
  26.6 0.6 %copy-done.2 = f32[128]{0:T(128)S(1)} copy-done((f32[128]{0:T(128)S(1)}, f32[128]{0:T(128)}, u32[]{:S(2)}) %copy-start.2) | copy-done | bytes 536
  27.3 0.0 copy-done.11
  27.3 0.0 copy-done.12
  27.3 26.6 %solve.1 = (f32[1,32]{1,0:T(1,128)}, f32[32,256]{1,0:T(8,128)}, f32[2,256]{1,0:T(2,128)S(1)}) custom-call(s32[2]{0:T(128)S(1)} %pad_add_fusion.place_ref, f32[32,8,128]{2,1,0:T(8,128)S(1)} %all-to-all-done.stats_ref, f32[1,128]{1,0:T(1,128)S(1)} %bitcast.391, f32[1,128]{1,0:T(1,128)S(1)} %bitcast.399, f32[1,128]{1,0:T(1,128)S(1)} %bitcast.400), custom_call_target="tpu_custom_call" | custom-call | tf_op jit(solution)/shard_map/solve/pallas_call | solution.py:384
  53.9 0.1 reduce_sum.41
  54.1 0.6 %fusion.85 = (f32[1]{0:T(128)}, f32[1]{0:T(128)}) fusion(f32[2]{0:T(128)S(1)} %reduce_sum.41), kind=kLoop, calls=%fused_computation.206 | loop fusion | bytes 16 | tf_op jit(solution)/shard_map/slice | solution.py:493
  55.9 0.2 conditional.1
Async XLA Ops:
  4.9 21.8 %all-to-all-start = ((f32[32,8,128]{2,1,0:T(8,128)}), f32[32,8,128]{2,1,0:T(8,128)S(1)}, u32[]{:S(2)}, u32[]{:S(2)}) async-start(f32[32,8,128]{2,1,0:T(8,128)} %broadcast_in_dim.155), calls=%async_computation | async-start | bytes 262144 | tf_op jit(solution)/shard_map/all_to_all | solution.py:488
  26.6 0.7 %copy-start.2 = (f32[128]{0:T(128)S(1)}, f32[128]{0:T(128)}, u32[]{:S(2)}) copy-start(f32[128]{0:T(128)} %param.23) | copy-start | bytes 1540
  26.6 0.7 %copy-start.11 = (f32[128]{0:T(128)S(1)}, f32[128]{0:T(128)}, u32[]{:S(2)}) copy-start(f32[128]{0:T(128)} %param.24) | copy-start | bytes 1540
  26.6 0.7 %copy-start.12 = (f32[128]{0:T(128)S(1)}, f32[128]{0:T(128)}, u32[]{:S(2)}) copy-start(f32[128]{0:T(128)} %param.25) | copy-start | bytes 1540

commit v2 on v1

--- a/solution.py
+++ b/solution.py
@@ -102,12 +102,14 @@
     imag_obs = pltpu.roll(waves[LOW:, MODES:], MODES - 1, 1)
     turned = (pltpu.roll(real, 1, 1), pltpu.roll(-imag, 1, 1))
     sources = ((real, imag), turned, (real, -imag), (real_obs, imag_obs))
+    rows = []
     for kind, (re, im) in enumerate(sources):
         cosine, sine = twiddle_ref[2 * kind], twiddle_ref[2 * kind + 1]
-        out_ref[2 * kind : 2 * kind + 1, :] = jnp.sum(re * cosine - im * sine, 0, keepdims=True)
-        out_ref[2 * kind + 1 : 2 * kind + 2, :] = jnp.sum(
-            re * sine + im * cosine, 0, keepdims=True
-        )
+        rows.append(jnp.sum(re * cosine - im * sine, 0, keepdims=True))
+        rows.append(jnp.sum(re * sine + im * cosine, 0, keepdims=True))
+    tile = jnp.concatenate(rows, axis=0)
+    for copy in range(out_ref.shape[0]):
+        out_ref[copy] = tile
 
 
 def toeplitz(ahead, behind):
@@ -468,12 +470,12 @@
     return mean[None], exact_dot(mine, back, NT)
 
 
-def statistics(site_row, obs_row, count):
+def statistics(site_row, obs_row, count, copies):
     transform, twiddles = tables()
     vmem = pl.BlockSpec(memory_space=pltpu.VMEM)
     return pl.pallas_call(
         statistics_kernel,
-        out_shape=jax.ShapeDtypeStruct((8, MODES), jnp.float32),
+        out_shape=jax.ShapeDtypeStruct((copies, 8, MODES), jnp.float32),
         in_specs=[pl.BlockSpec(memory_space=pltpu.SMEM)] + [vmem] * 4,
         out_specs=vmem,
         name="statistics",
@@ -483,8 +485,7 @@
 def local(observations, site_ids, counts, frequencies, decay, proc_var):
     steps = lax.axis_size("tm")
     block = WIDTH // lax.axis_size("rows")
-    stats = statistics(site_ids, observations, counts)
-    copies = jnp.broadcast_to(stats, (steps, *stats.shape))
+    copies = statistics(site_ids, observations, counts, steps)
     everyone = lax.all_to_all(copies, "tm", split_axis=0, concat_axis=0, tiled=True)
     place = jnp.stack([lax.axis_index("tm"), lax.axis_index("rows")]).astype(jnp.int32)
     mean, cov, check = solve(place, everyone, frequencies, decay, proc_var, block)

time: 56.6 us -> 55.3 us (0.977)
  local copies, waits for them, and re-layouts: 2.63 us -> 1.29 us
    broadcast_in_dim x1 -> x0, local copies, waits for them, and re-layouts: 1.34 us -> none  [local(): copies = jnp.broadcast_to(stats, (steps, *stats.shape))]
where the time goes in v2:
time: 55.3 us; the launch traced here: 55.1 us
  Pallas kernels  28.9 us (52%)
  starting transfers between devices  11.3 us (20%)
  waiting for transfers between devices  10.4 us (19%)
  between operations  2.74 us (5%)
  local copies, waits for them, and re-layouts  1.29 us (2%)
    pallas_call x1, Pallas kernels, solve(): pl.pallas_call(solve_kernel, out_shape=(jax.ShapeDtypeStruct((1, block),...  26.6 us
    all_to_all x1, starting transfers between devices, local(): lax.all_to_all(copies, 'tm', split_axis=0, concat_axis=0, tiled=True)  11.3 us
    all_to_all x1, waiting for transfers between devices, local(): lax.all_to_all(copies, 'tm', split_axis=0, concat_axis=0, tiled=True)  10.4 us
    pallas_call x1, Pallas kernels, statistics(): pl.pallas_call(statistics_kernel, out_shape=jax.ShapeDtypeStruct((copies,...  2.3 us
  transfers between devices with their start and end apart: 1, of which 1 were waited for; matrix products, arithmetic and copies ran while one was open for 0% of the time, Pallas kernels for 0%

profile of v2, /device:TPU:16, one launch (start us, length us, event | category | flops | bytes accessed | tf_op | source)
XLA Modules:
  0.0 55.1 jit_solution(15137611888337491115)
XLA Ops:
  1.3 2.3 %statistics.1 = f32[32,8,128]{2,1,0:T(8,128)} custom-call(s32[1]{0:T(128)S(6)} %copy.79.count_ref, s32[1,2048]{1,0:T(1,128)} %site_ref.1, f32[1,2048]{1,0:T(1,128)} %obs_ref.1, f32[128,256]{1,0:T(8,128)} %constant.167.clone.transform_ref, f32[8,32,128]{2,1,0:T(8,128)} %constant.168.clone.twiddle_ref), custom_call_target="tpu_custom_call" | custom-call | tf_op jit(solution)/shard_map/statistics/pallas_call | solution.py:476
  3.6 11.3 %all-to-all-start = ((f32[32,8,128]{2,1,0:T(8,128)}), f32[32,8,128]{2,1,0:T(8,128)S(1)}, u32[]{:S(2)}, u32[]{:S(2)}) async-start(f32[32,8,128]{2,1,0:T(8,128)} %statistics.1), calls=%async_computation | async-start | bytes 262144 | tf_op jit(solution)/shard_map/all_to_all | solution.py:489
  14.9 0.1 pad_add_fusion.place_ref
  15.0 10.4 %all-to-all-done.stats_ref = f32[32,8,128]{2,1,0:T(8,128)S(1)} async-done(((f32[32,8,128]{2,1,0:T(8,128)}), f32[32,8,128]{2,1,0:T(8,128)S(1)}, u32[]{:S(2)}, u32[]{:S(2)}) %all-to-all-start) | async-done | bytes 131104 | tf_op jit(solution)/shard_map/all_to_all | solution.py:489
  25.3 0.0 copy-start.2
  25.3 0.0 copy-start.11
  25.4 0.0 copy-start.12
  25.4 0.6 %copy-done.2 = f32[128]{0:T(128)S(1)} copy-done((f32[128]{0:T(128)S(1)}, f32[128]{0:T(128)}, u32[]{:S(2)}) %copy-start.2) | copy-done | bytes 536
  26.0 0.0 copy-done.11
  26.0 0.0 copy-done.12
  26.0 26.6 %solve.1 = (f32[1,32]{1,0:T(1,128)}, f32[32,256]{1,0:T(8,128)}, f32[2,256]{1,0:T(2,128)S(1)}) custom-call(s32[2]{0:T(128)S(1)} %pad_add_fusion.place_ref, f32[32,8,128]{2,1,0:T(8,128)S(1)} %all-to-all-done.stats_ref, f32[1,128]{1,0:T(1,128)S(1)} %bitcast.391, f32[1,128]{1,0:T(1,128)S(1)} %bitcast.399, f32[1,128]{1,0:T(1,128)S(1)} %bitcast.400), custom_call_target="tpu_custom_call" | custom-call | tf_op jit(solution)/shard_map/solve/pallas_call | solution.py:386
  52.7 0.1 reduce_sum.41
  52.8 0.6 %fusion.85 = (f32[1]{0:T(128)}, f32[1]{0:T(128)}) fusion(f32[2]{0:T(128)S(1)} %reduce_sum.41), kind=kLoop, calls=%fused_computation.206 | loop fusion | bytes 16 | tf_op jit(solution)/shard_map/slice | solution.py:494
  54.7 0.2 conditional.1
Async XLA Ops:
  3.6 21.8 %all-to-all-start = ((f32[32,8,128]{2,1,0:T(8,128)}), f32[32,8,128]{2,1,0:T(8,128)S(1)}, u32[]{:S(2)}, u32[]{:S(2)}) async-start(f32[32,8,128]{2,1,0:T(8,128)} %statistics.1), calls=%async_computation | async-start | bytes 262144 | tf_op jit(solution)/shard_map/all_to_all | solution.py:489
  25.3 0.7 %copy-start.2 = (f32[128]{0:T(128)S(1)}, f32[128]{0:T(128)}, u32[]{:S(2)}) copy-start(f32[128]{0:T(128)} %param.23) | copy-start | bytes 1540
  25.3 0.7 %copy-start.11 = (f32[128]{0:T(128)S(1)}, f32[128]{0:T(128)}, u32[]{:S(2)}) copy-start(f32[128]{0:T(128)} %param.24) | copy-start | bytes 1540
  25.4 0.7 %copy-start.12 = (f32[128]{0:T(128)S(1)}, f32[128]{0:T(128)}, u32[]{:S(2)}) copy-start(f32[128]{0:T(128)} %param.25) | copy-start | bytes 1540

commit v3 on v2

--- a/solution.py
+++ b/solution.py
@@ -238,7 +238,7 @@
     variance_ref,
     mean_ref,
     cov_ref,
-    check_ref,
+    flag_ref,
     phase_ref,
     block1_ref,
     block2_ref,
@@ -251,6 +251,7 @@
     carried_ref,
     rows_ref,
     columns_ref,
+    check_ref,
 ):
     steps = stats_ref.shape[0]
     half = steps // 2
@@ -377,6 +378,8 @@
         return call
 
     run(noted(chain_inverse, 0), noted(final_inverse, 1), noted(final_rows, 1), product3)
+    chain, final = jnp.sum(check_ref[0:1, :]), jnp.sum(check_ref[1:2, :])
+    flag_ref[0] = jnp.where((chain <= CHAIN_LIMIT) & (final <= FINAL_LIMIT), 1, 0)
 
 
 def solve(place, stats, frequencies, decay, proc_var, block):
@@ -388,10 +391,10 @@
         out_shape=(
             jax.ShapeDtypeStruct((1, block), jnp.float32),
             jax.ShapeDtypeStruct((block, WIDTH), jnp.float32),
-            jax.ShapeDtypeStruct((2, WIDTH), jnp.float32),
+            jax.ShapeDtypeStruct((1,), jnp.int32),
         ),
         in_specs=[pl.BlockSpec(memory_space=pltpu.SMEM)] + [vmem] * 4,
-        out_specs=(vmem, vmem, vmem),
+        out_specs=(vmem, vmem, pl.BlockSpec(memory_space=pltpu.SMEM)),
         scratch_shapes=[
             pltpu.VMEM((stats.shape[0], 8, MODES), jnp.float32),
             *[square] * 7,
@@ -399,6 +402,7 @@
             tall,
             pltpu.VMEM((40, WIDTH), jnp.float32),
             pltpu.VMEM((WIDTH, 8), jnp.float32),
+            pltpu.VMEM((2, WIDTH), jnp.float32),
         ],
         compiler_params=pltpu.CompilerParams(vmem_limit_bytes=48 << 20),
         name="solve",
@@ -488,10 +492,9 @@
     copies = statistics(site_ids, observations, counts, steps)
     everyone = lax.all_to_all(copies, "tm", split_axis=0, concat_axis=0, tiled=True)
     place = jnp.stack([lax.axis_index("tm"), lax.axis_index("rows")]).astype(jnp.int32)
-    mean, cov, check = solve(place, everyone, frequencies, decay, proc_var, block)
-    measure = jnp.sum(check, axis=1)
+    mean, cov, flag = solve(place, everyone, frequencies, decay, proc_var, block)
     mean, cov = lax.cond(
-        (measure[0] <= CHAIN_LIMIT) & (measure[1] <= FINAL_LIMIT),
+        flag[0] == 1,
         lambda place, everyone, mean, cov: (mean, cov),
         lambda place, everyone, mean, cov: general(
             place, everyone, frequencies, decay, proc_var, block

time: 55.3 us -> 53.8 us (0.973)
  between operations: 2.74 us -> 2.04 us
  local copies, waits for them, and re-layouts: 1.29 us -> 0.68 us
    slice x1 -> x0, local copies, waits for them, and re-layouts: 0.61 us -> none  [local(): measure[1] <= FINAL_LIMIT]
where the time goes in v3:
time: 53.8 us; the launch traced here: 53.6 us
  Pallas kernels  28.9 us (54%)
  starting transfers between devices  11.3 us (21%)
  waiting for transfers between devices  10.4 us (19%)
  between operations  2.04 us (4%)
  local copies, waits for them, and re-layouts  0.68 us (1%)
    pallas_call x1, Pallas kernels, solve(): pl.pallas_call(solve_kernel, out_shape=(jax.ShapeDtypeStruct((1, block),...  26.6 us
    all_to_all x1, starting transfers between devices, local(): lax.all_to_all(copies, 'tm', split_axis=0, concat_axis=0, tiled=True)  11.3 us
    all_to_all x1, waiting for transfers between devices, local(): lax.all_to_all(copies, 'tm', split_axis=0, concat_axis=0, tiled=True)  10.4 us
    pallas_call x1, Pallas kernels, statistics(): pl.pallas_call(statistics_kernel, out_shape=jax.ShapeDtypeStruct((copies,...  2.3 us
  transfers between devices with their start and end apart: 1, of which 1 were waited for; matrix products, arithmetic and copies ran while one was open for 0% of the time, Pallas kernels for 0%

profile of v3, /device:TPU:16, one launch (start us, length us, event | category | flops | bytes accessed | tf_op | source)
XLA Modules:
  0.0 53.6 jit_solution(8743452285666549137)
XLA Ops:
  1.3 2.3 %statistics.1 = f32[32,8,128]{2,1,0:T(8,128)} custom-call(s32[1]{0:T(128)S(6)} %copy.79.count_ref, s32[1,2048]{1,0:T(1,128)} %site_ref.1, f32[1,2048]{1,0:T(1,128)} %obs_ref.1, f32[128,256]{1,0:T(8,128)} %constant.162.clone.transform_ref, f32[8,32,128]{2,1,0:T(8,128)} %constant.163.clone.twiddle_ref), custom_call_target="tpu_custom_call" | custom-call | tf_op jit(solution)/shard_map/statistics/pallas_call | solution.py:480
  3.6 11.3 %all-to-all-start = ((f32[32,8,128]{2,1,0:T(8,128)}), f32[32,8,128]{2,1,0:T(8,128)S(1)}, u32[]{:S(2)}, u32[]{:S(2)}) async-start(f32[32,8,128]{2,1,0:T(8,128)} %statistics.1), calls=%async_computation | async-start | bytes 262144 | tf_op jit(solution)/shard_map/all_to_all | solution.py:493
  14.9 0.1 pad_add_fusion.place_ref
  15.0 10.4 %all-to-all-done.stats_ref = f32[32,8,128]{2,1,0:T(8,128)S(1)} async-done(((f32[32,8,128]{2,1,0:T(8,128)}), f32[32,8,128]{2,1,0:T(8,128)S(1)}, u32[]{:S(2)}, u32[]{:S(2)}) %all-to-all-start) | async-done | bytes 131104 | tf_op jit(solution)/shard_map/all_to_all | solution.py:493
  25.4 0.0 copy-start.2
  25.4 0.0 copy-start.11
  25.4 0.0 copy-start.12
  25.4 0.6 %copy-done.2 = f32[128]{0:T(128)S(1)} copy-done((f32[128]{0:T(128)S(1)}, f32[128]{0:T(128)}, u32[]{:S(2)}) %copy-start.2) | copy-done | bytes 536
  26.0 0.0 copy-done.11
  26.0 0.0 copy-done.12
  26.0 26.6 %solve.1 = (f32[1,32]{1,0:T(1,128)}, f32[32,256]{1,0:T(8,128)}, s32[1]{0:T(128)}) custom-call(s32[2]{0:T(128)S(1)} %pad_add_fusion.place_ref, f32[32,8,128]{2,1,0:T(8,128)S(1)} %all-to-all-done.stats_ref, f32[1,128]{1,0:T(1,128)S(1)} %bitcast.391, f32[1,128]{1,0:T(1,128)S(1)} %bitcast.399, f32[1,128]{1,0:T(1,128)S(1)} %bitcast.400), custom_call_target="tpu_custom_call" | custom-call | tf_op jit(solution)/shard_map/solve/pallas_call | solution.py:389
  53.2 0.2 conditional.1
Async XLA Ops:
  3.6 21.8 %all-to-all-start = ((f32[32,8,128]{2,1,0:T(8,128)}), f32[32,8,128]{2,1,0:T(8,128)S(1)}, u32[]{:S(2)}, u32[]{:S(2)}) async-start(f32[32,8,128]{2,1,0:T(8,128)} %statistics.1), calls=%async_computation | async-start | bytes 262144 | tf_op jit(solution)/shard_map/all_to_all | solution.py:493
  25.4 0.7 %copy-start.2 = (f32[128]{0:T(128)S(1)}, f32[128]{0:T(128)}, u32[]{:S(2)}) copy-start(f32[128]{0:T(128)} %param.23) | copy-start | bytes 1540
  25.4 0.7 %copy-start.11 = (f32[128]{0:T(128)S(1)}, f32[128]{0:T(128)}, u32[]{:S(2)}) copy-start(f32[128]{0:T(128)} %param.24) | copy-start | bytes 1540
  25.4 0.7 %copy-start.12 = (f32[128]{0:T(128)S(1)}, f32[128]{0:T(128)}, u32[]{:S(2)}) copy-start(f32[128]{0:T(128)} %param.25) | copy-start | bytes 1540

commit v4 on v3

--- a/solution.py
+++ b/solution.py
@@ -334,12 +334,12 @@
 
         def body(index, _):
             excess1, excess2, _, _ = advance(index)
+            rows_ref[8:9, :] = build(index + 1, block1_ref)
+            rows_ref[16:17, :] = build(second_node(index + 1), block2_ref)
             next1 = invert_chain(excess1, base, damping, mask)
             next2 = invert_chain(excess2, base, damping, mask)
             rest1_ref[...], rows_ref[32:33, :], lost1_ref[...] = next1
             rest2_ref[...], rows_ref[33:34, :], lost2_ref[...] = next2
-            rows_ref[8:9, :] = build(index + 1, block1_ref)
-            rows_ref[16:17, :] = build(second_node(index + 1), block2_ref)
             return 0
 
         lax.fori_loop(0, half - 1, body, 0)

time: 53.8 us -> 53.9 us (level)
  no operation moved by 1% of the time
where the time goes in v4:
time: 53.9 us; the launch traced here: 53.7 us
  Pallas kernels  29 us (54%)
  starting transfers between devices  11.3 us (21%)
  waiting for transfers between devices  10.4 us (19%)
  between operations  2.04 us (4%)
  local copies, waits for them, and re-layouts  0.68 us (1%)
    pallas_call x1, Pallas kernels, solve(): pl.pallas_call(solve_kernel, out_shape=(jax.ShapeDtypeStruct((1, block),...  26.7 us
    all_to_all x1, starting transfers between devices, local(): lax.all_to_all(copies, 'tm', split_axis=0, concat_axis=0, tiled=True)  11.3 us
    all_to_all x1, waiting for transfers between devices, local(): lax.all_to_all(copies, 'tm', split_axis=0, concat_axis=0, tiled=True)  10.4 us
    pallas_call x1, Pallas kernels, statistics(): pl.pallas_call(statistics_kernel, out_shape=jax.ShapeDtypeStruct((copies,...  2.3 us
  transfers between devices with their start and end apart: 1, of which 1 were waited for; matrix products, arithmetic and copies ran while one was open for 0% of the time, Pallas kernels for 0%

profile of v4, /device:TPU:16, one launch (start us, length us, event | category | flops | bytes accessed | tf_op | source)
XLA Modules:
  0.0 53.7 jit_solution(3805902967342954329)
XLA Ops:
  1.3 2.3 %statistics.1 = f32[32,8,128]{2,1,0:T(8,128)} custom-call(s32[1]{0:T(128)S(6)} %copy.79.count_ref, s32[1,2048]{1,0:T(1,128)} %site_ref.1, f32[1,2048]{1,0:T(1,128)} %obs_ref.1, f32[128,256]{1,0:T(8,128)} %constant.162.clone.transform_ref, f32[8,32,128]{2,1,0:T(8,128)} %constant.163.clone.twiddle_ref), custom_call_target="tpu_custom_call" | custom-call | tf_op jit(solution)/shard_map/statistics/pallas_call | solution.py:480
  3.6 11.3 %all-to-all-start = ((f32[32,8,128]{2,1,0:T(8,128)}), f32[32,8,128]{2,1,0:T(8,128)S(1)}, u32[]{:S(2)}, u32[]{:S(2)}) async-start(f32[32,8,128]{2,1,0:T(8,128)} %statistics.1), calls=%async_computation | async-start | bytes 262144 | tf_op jit(solution)/shard_map/all_to_all | solution.py:493
  14.9 0.1 pad_add_fusion.place_ref
  15.0 10.4 %all-to-all-done.stats_ref = f32[32,8,128]{2,1,0:T(8,128)S(1)} async-done(((f32[32,8,128]{2,1,0:T(8,128)}), f32[32,8,128]{2,1,0:T(8,128)S(1)}, u32[]{:S(2)}, u32[]{:S(2)}) %all-to-all-start) | async-done | bytes 131104 | tf_op jit(solution)/shard_map/all_to_all | solution.py:493
  25.4 0.0 copy-start.2
  25.4 0.0 copy-start.11
  25.4 0.0 copy-start.12
  25.4 0.6 %copy-done.2 = f32[128]{0:T(128)S(1)} copy-done((f32[128]{0:T(128)S(1)}, f32[128]{0:T(128)}, u32[]{:S(2)}) %copy-start.2) | copy-done | bytes 536
  26.0 0.0 copy-done.11
  26.0 0.0 copy-done.12
  26.0 26.7 %solve.1 = (f32[1,32]{1,0:T(1,128)}, f32[32,256]{1,0:T(8,128)}, s32[1]{0:T(128)}) custom-call(s32[2]{0:T(128)S(1)} %pad_add_fusion.place_ref, f32[32,8,128]{2,1,0:T(8,128)S(1)} %all-to-all-done.stats_ref, f32[1,128]{1,0:T(1,128)S(1)} %bitcast.391, f32[1,128]{1,0:T(1,128)S(1)} %bitcast.399, f32[1,128]{1,0:T(1,128)S(1)} %bitcast.400), custom_call_target="tpu_custom_call" | custom-call | tf_op jit(solution)/shard_map/solve/pallas_call | solution.py:389
  53.3 0.2 conditional.1
Async XLA Ops:
  3.6 21.8 %all-to-all-start = ((f32[32,8,128]{2,1,0:T(8,128)}), f32[32,8,128]{2,1,0:T(8,128)S(1)}, u32[]{:S(2)}, u32[]{:S(2)}) async-start(f32[32,8,128]{2,1,0:T(8,128)} %statistics.1), calls=%async_computation | async-start | bytes 262144 | tf_op jit(solution)/shard_map/all_to_all | solution.py:493
  25.4 0.7 %copy-start.2 = (f32[128]{0:T(128)S(1)}, f32[128]{0:T(128)}, u32[]{:S(2)}) copy-start(f32[128]{0:T(128)} %param.23) | copy-start | bytes 1540
  25.4 0.7 %copy-start.11 = (f32[128]{0:T(128)S(1)}, f32[128]{0:T(128)}, u32[]{:S(2)}) copy-start(f32[128]{0:T(128)} %param.24) | copy-start | bytes 1540
  25.4 0.7 %copy-start.12 = (f32[128]{0:T(128)S(1)}, f32[128]{0:T(128)}, u32[]{:S(2)}) copy-start(f32[128]{0:T(128)} %param.25) | copy-start | bytes 1540
